TPU v7x, 32 devices: a whole 2x2x4 slice. The times are simulated.
32 devices in a mesh: batch: 4 (over y, core), proto: 8 (over z, x).
Axes of the slice: x: 2, y: 2, z: 4, core: 2. Of those that a mesh axis runs over, the one named last changes fastest.
Arguments:
- features: bfloat16 [4096, 256], P(('batch', 'proto')), may hold values from -8 to 8
- head_weight: bfloat16 [256, 65536], P('batch', 'proto'), may hold values from -0.375 to 0.375
- student_scores: bfloat16 [2, 4096, 65536], P(None, 'batch', 'proto'), may hold values from -1 to 1
Outputs:
- targets: bfloat16 [4096, 65536], P('batch', 'proto')
- row_loss: float32 [2, 4096], P(None, 'batch')
All inputs are finite; a program needn't handle non-finite values.
Results may differ from a plain program's by a relative error of at most 0.0013.
Values may be sent and summed in bfloat16 or wider, within the bound.
No kernel may reach another device: no remote copies, remote signals or barrier semaphores. Data moves between devices by JAX's collectives and lax.ppermute only.
A program may use at most 192 MiB of HBM per device.

v0:
```python
import jax
import jax.numpy as jnp
from jax import lax
from jax.sharding import PartitionSpec as P

PROTOS = 65536
ITERS = 3
TEACHER_TEMP = 0.07
STUDENT_TEMP = 0.1


def normalize_columns(balance):
    column_sum = lax.psum(jnp.sum(balance, axis=0), "batch")
    return balance / column_sum[None, :]


def crop_totals(balance):
    return lax.psum(jnp.sum(balance, axis=1), "proto")


def local(features, head_weight, student_scores):
    gathered = lax.all_gather(features, "proto", axis=0, tiled=True)
    feat_wide = gathered.astype(jnp.float32)
    fnorm = jnp.sqrt(jnp.sum(feat_wide * feat_wide, axis=1) + 1e-06)
    piece = lax.all_gather(head_weight, "batch", axis=0, tiled=True)
    piece_wide = piece.astype(jnp.float32)
    raw = jnp.dot(gathered, piece, preferred_element_type=jnp.float32)
    squares = jnp.sum(piece_wide * piece_wide, axis=0)
    wnorm = jnp.sqrt(squares + 1e-06)
    balance = jnp.exp(raw / (fnorm[:, None] * wnorm[None, :]) / TEACHER_TEMP)
    logits = student_scores.astype(jnp.float32) / STUDENT_TEMP
    exp_sums = jnp.sum(jnp.exp(logits), axis=2)
    for step in range(ITERS - 1):
        balance = normalize_columns(balance)
        balance = balance / crop_totals(balance)[:, None]
    balance = normalize_columns(balance)
    weighted = jnp.sum(logits * balance[None, :, :], axis=2)
    last_rows, total_exp, total_weighted = lax.psum(
        (jnp.sum(balance, axis=1), exp_sums, weighted), "proto"
    )
    balance = balance / last_rows[:, None]
    row_loss = jnp.log(total_exp) - total_weighted / last_rows[None, :]
    targets = (balance * PROTOS).astype(jnp.bfloat16)
    return (targets, row_loss)


def solution(mesh):
    return jax.shard_map(
        local,
        mesh=mesh,
        in_specs=(P(("batch", "proto"), None), P("batch", "proto"), P(None, "batch", "proto")),
        out_specs=(P("batch", "proto"), P(None, "batch")),
        check_vma=False,
    )
```

profile of v0, /device:TPU:0, one launch (start us, length us, event | category | flops | bytes accessed | tf_op | source)
XLA Modules:
  0.0 311.4 jit_solution(16653263350034114309)
XLA Ops:
  7.2 0.0 all-gather.2.cloned.1.call-start
  7.2 0.7 all-gather.2.cloned.1.call-update
  7.9 33.2 %all_gather.6 = bf16[1024,256]{1,0:T(8,128)(2,1)S(1)} all-gather(bf16[128,256]{1,0:T(8,128)(2,1)} %param.3), channel_id=1, replica_groups=mesh['batch'=4,'proto'=8] {'proto'}, dimensions={0}, use_global_device_ids=true | all-gather | bytes 589824 | tf_op jit(solution)/shard_map/all_gather | solution.py:22
  41.1 0.2 multiply_reduce_fusion.1
  41.4 5.4 %all-gather.2.cloned.1.call-done = bf16[256,8192]{1,0:T(8,128)(2,1)} async-done(((bf16[64,8192]{1,0:T(8,128)(2,1)}), bf16[256,8192]{1,0:T(8,128)(2,1)}) %all-gather.2.cloned.1.call-update) | async-done | bytes 4194320 | tf_op jit(solution)/shard_map/all_gather | solution.py:25
  46.7 3.1 multiply_reduce_fusion
  49.8 17.7 %fusion.16 = (f32[8192]{0:T(1024)S(1)}, f32[1024,8192]{1,0:T(8,128)}) fusion(f32[8192]{0:T(1024)S(1)} %add_sqrt_fusion, f32[1024]{0:T(1024)S(1)} %add_sqrt_fusion.1, bf16[1024,256]{1,0:T(8,128)(2,1)S(1)} %all_gather.6, bf16[256,8192]{1,0:T(8,128)(2,1)} %all-gather.2.cloned.1.call-done), kind=kOutput, calls=%fused_computation.28 | convolution fusion | flops 4328513536 | bytes 38342656 | tf_op jit(solution)/shard_map/dot_general | solution.py:27
  67.5 10.4 %psum.56 = f32[8192]{0:T(1024)S(1)} all-reduce(f32[8192]{0:T(1024)S(1)} %get-tuple-element.9), channel_id=1, replica_groups=mesh['batch'=4,'proto'=8] {'batch'}, use_global_device_ids=true, to_apply=%region_3.0 | all-reduce | flops 8192 | bytes 65536 | tf_op jit(solution)/shard_map/psum | solution.py:13
  77.9 12.2 %divide_reduce_fusion = f32[1024]{0:T(1024)S(1)} fusion(f32[1024,8192]{1,0:T(8,128)} %get-tuple-element.10, f32[8192]{0:T(1024)S(1)} %psum.56), kind=kLoop, calls=%fused_computation.16 | loop fusion | flops 16776192 | bytes 33591296 | tf_op jit(solution)/shard_map/reduce_sum | solution.py:18
  90.1 21.5 %psum.57 = f32[1024]{0:T(1024)S(1)} all-reduce(f32[1024]{0:T(1024)S(1)} %divide_reduce_fusion), channel_id=1, replica_groups=mesh['batch'=4,'proto'=8] {'proto'}, use_global_device_ids=true, to_apply=%region_5.0 | all-reduce | flops 1024 | bytes 8192 | tf_op jit(solution)/shard_map/psum | solution.py:18
  111.6 14.1 %fusion.11 = f32[8192]{0:T(1024)S(1)} fusion(f32[1024,8192]{1,0:T(8,128)} %get-tuple-element.10, f32[1024]{0:T(1024)S(1)} %psum.57, f32[8192]{0:T(1024)S(1)} %psum.56), kind=kLoop, calls=%fused_computation.17 | loop fusion | flops 25157632 | bytes 33624064 | tf_op jit(solution)/shard_map/reduce_sum | solution.py:13
  125.7 10.3 %psum.58 = f32[8192]{0:T(1024)S(1)} all-reduce(f32[8192]{0:T(1024)S(1)} %fusion.11), channel_id=1, replica_groups=mesh['batch'=4,'proto'=8] {'batch'}, use_global_device_ids=true, to_apply=%region_7.0 | all-reduce | flops 8192 | bytes 65536 | tf_op jit(solution)/shard_map/psum | solution.py:13
  136.0 14.1 %fusion.13 = f32[1024]{0:T(1024)S(1)} fusion(f32[1024,8192]{1,0:T(8,128)} %get-tuple-element.10, f32[8192]{0:T(1024)S(1)} %psum.58, f32[1024]{0:T(1024)S(1)} %psum.57, f32[8192]{0:T(1024)S(1)} %psum.56), kind=kLoop, calls=%fused_computation.19 | loop fusion | flops 33553408 | bytes 33628160 | tf_op jit(solution)/shard_map/reduce_sum | solution.py:18
  150.1 17.1 %psum.59 = f32[1024]{0:T(1024)S(1)} all-reduce(f32[1024]{0:T(1024)S(1)} %fusion.13), channel_id=1, replica_groups=mesh['batch'=4,'proto'=8] {'proto'}, use_global_device_ids=true, to_apply=%region_9.0 | all-reduce | flops 1024 | bytes 8192 | tf_op jit(solution)/shard_map/psum | solution.py:18
  167.3 14.5 %fusion.14 = f32[8192]{0:T(1024)S(1)} fusion(f32[1024,8192]{1,0:T(8,128)} %get-tuple-element.10, f32[1024]{0:T(1024)S(1)} %psum.59, f32[8192]{0:T(1024)S(1)} %psum.58, f32[1024]{0:T(1024)S(1)} %psum.57, f32[8192]{0:T(1024)S(1)} %psum.56), kind=kLoop, calls=%fused_computation.20 | loop fusion | flops 41934848 | bytes 33660928 | tf_op jit(solution)/shard_map/reduce_sum | solution.py:13
  181.7 10.4 %psum.60 = f32[8192]{0:T(1024)S(1)} all-reduce(f32[8192]{0:T(1024)S(1)} %fusion.14), channel_id=1, replica_groups=mesh['batch'=4,'proto'=8] {'batch'}, use_global_device_ids=true, to_apply=%region_11.0 | all-reduce | flops 8192 | bytes 65536 | tf_op jit(solution)/shard_map/psum | solution.py:13
  192.2 28.0 %broadcast_multiply_fusion = (f32[1024,8192]{1,0:T(8,128)}, f32[1024]{0:T(1024)S(1)}) fusion(f32[1024,8192]{1,0:T(8,128)} %get-tuple-element.10, f32[8192]{0:T(1024)S(1)} %psum.60, f32[1024]{0:T(1024)S(1)} %psum.59, f32[8192]{0:T(1024)S(1)} %psum.58, f32[1024]{0:T(1024)S(1)} %psum.57, f32[8192]{0:T(1024)S(1)} %psum.56), kind=kLoop, calls=%fused_computation.21 | loop fusion | flops 58719232 | bytes 67219456 | tf_op jit(solution)/shard_map/mul | solution.py:37
  220.2 27.8 %fusion.1 = (f32[2,1024]{1,0:T(2,128)S(1)}, f32[2,1024]{1,0:T(2,128)S(1)}) fusion(bf16[2,1024,8192]{2,1,0:T(8,128)(2,1)} %param.5, f32[1024,8192]{1,0:T(8,128)} %get-tuple-element.7), kind=kLoop, calls=%fused_computation.3 | loop fusion | flops 83881984 | bytes 67125248 | tf_op jit(solution)/shard_map/reduce_sum | solution.py:32
  248.0 34.9 %all-reduce = (f32[1024]{0:T(1024)S(1)}, f32[2,1024]{1,0:T(2,128)S(1)}, f32[2,1024]{1,0:T(2,128)S(1)}) all-reduce(f32[1024]{0:T(1024)S(1)} %get-tuple-element.8, f32[2,1024]{1,0:T(2,128)S(1)} %get-tuple-element.3, f32[2,1024]{1,0:T(2,128)S(1)} %get-tuple-element.2), channel_id=1, replica_groups=mesh['batch'=4,'proto'=8] {'proto'}, use_global_device_ids=true, to_apply=%region_13.0 | all-reduce | flops 5120 | bytes 40960 | tf_op jit(solution)/shard_map/psum | solution.py:38
  282.9 21.1 %fusion.12 = bf16[1024,8192]{1,0:T(8,128)(2,1)} fusion(f32[1024,8192]{1,0:T(8,128)} %get-tuple-element.10, f32[1024]{0:T(1024)S(1)} %get-tuple-element.4, f32[8192]{0:T(1024)S(1)} %psum.60, f32[1024]{0:T(1024)S(1)} %psum.59, f32[8192]{0:T(1024)S(1)} %psum.58, f32[1024]{0:T(1024)S(1)} %psum.57, f32[8192]{0:T(1024)S(1)} %psum.56), kind=kLoop, calls=%fused_computation.18 | loop fusion | flops 67108864 | bytes 50442240 | tf_op jit(solution)/shard_map/convert_element_type | solution.py:43
  303.9 0.6 divide_subtract_fusion
  (2 shorter events, 0.0 us)
Async XLA Ops:
  7.2 39.6 %all-gather.2.cloned.1.call-start = ((), (), s32[]{:S(2)}) async-start(), calls=%async_computation | async-start | bytes 5242880 | tf_op jit(solution)/shard_map/all_gather | solution.py:25
Sparse Core Ops, SparseCore 0:
  9.5 37.1 all-gather.1
where the time goes:
time: 312 us; the launch traced here: 311 us
  blocking collectives  138 us (44%)
  other arithmetic  136 us (44%)
  matrix products  17.7 us (6%)
  between operations  14.1 us (5%)
  waiting for transfers between devices  6.05 us (2%)
    psum x2, blocking collectives, crop_totals(): return lax.psum(jnp.sum(balance, axis=1), 'proto')  38.7 us
    psum x1, blocking collectives, local(): lax.psum((jnp.sum(balance, axis=1), exp_sums, weighted), 'proto')  34.9 us
    all_gather x1, blocking collectives, local(): gathered = lax.all_gather(features, 'proto', axis=0, tiled=True)  33.2 us
    psum x3, blocking collectives, normalize_columns(): column_sum = lax.psum(jnp.sum(balance, axis=0), 'batch')  31.1 us
    reduce_sum x2, other arithmetic, normalize_columns(): column_sum = lax.psum(jnp.sum(balance, axis=0), 'batch')  28.5 us
    mul x1, other arithmetic, local(): weighted = jnp.sum(logits * balance[None, :, :], axis=2)  28 us
    reduce_sum x1, other arithmetic, local(): exp_sums = jnp.sum(jnp.exp(logits), axis=2)  27.8 us
    reduce_sum x2, other arithmetic, crop_totals(): return lax.psum(jnp.sum(balance, axis=1), 'proto')  26.3 us
  transfers between devices with their start and end apart: 1, of which 1 were waited for; matrix products, arithmetic and copies ran while one was open for 0% of the time, Pallas kernels for 0%

commit v1 on v0

--- a/solution.py
+++ b/solution.py
@@ -9,13 +9,19 @@
 STUDENT_TEMP = 0.1
 
 
+def add_all(x, axis):
+    parts = lax.all_gather(x, axis, axis=0, tiled=False)
+    summed = parts.sum(axis=0)
+    return summed
+
+
 def normalize_columns(balance):
     column_sum = lax.psum(jnp.sum(balance, axis=0), "batch")
     return balance / column_sum[None, :]
 
 
 def crop_totals(balance):
-    return lax.psum(jnp.sum(balance, axis=1), "proto")
+    return add_all(jnp.sum(balance, axis=1), "proto")
 
 
 def local(features, head_weight, student_scores):

time: 312 us -> 337 us (1.080)
  blocking collectives: 138 us -> 163 us
    all_gather x0 -> x2, blocking collectives: none -> 61.4 us  [add_all(): parts = lax.all_gather(x, axis, axis=0, tiled=False)]
    psum x2 -> x0, blocking collectives: 38.7 us -> none  [crop_totals(): return lax.psum(jnp.sum(balance, axis=1), 'proto')]
    reduce_sum x2 -> x4, other arithmetic: 26.3 us -> 26.4 us  [the longest x2 26.3 us: crop_totals(): return add_all(jnp.sum(balance, axis=1), 'proto')]
where the time goes in v1:
time: 337 us; the launch traced here: 336 us
  blocking collectives  163 us (48%)
  other arithmetic  136 us (40%)
  matrix products  17.7 us (5%)
  between operations  14.1 us (4%)
  waiting for transfers between devices  6.05 us (2%)
    all_gather x2, blocking collectives, add_all(): parts = lax.all_gather(x, axis, axis=0, tiled=False)  61.4 us
    psum x1, blocking collectives, local(): lax.psum((jnp.sum(balance, axis=1), exp_sums, weighted), 'proto')  37 us
    all_gather x1, blocking collectives, local(): gathered = lax.all_gather(features, 'proto', axis=0, tiled=True)  33.2 us
    psum x3, blocking collectives, normalize_columns(): column_sum = lax.psum(jnp.sum(balance, axis=0), 'batch')  31.1 us
    reduce_sum x2, other arithmetic, normalize_columns(): column_sum = lax.psum(jnp.sum(balance, axis=0), 'batch')  28.5 us
    mul x1, other arithmetic, local(): weighted = jnp.sum(logits * balance[None, :, :], axis=2)  28 us
    reduce_sum x1, other arithmetic, local(): exp_sums = jnp.sum(jnp.exp(logits), axis=2)  27.8 us
    reduce_sum x2, other arithmetic, crop_totals(): return add_all(jnp.sum(balance, axis=1), 'proto')  26.3 us
  transfers between devices with their start and end apart: 1, of which 1 were waited for; matrix products, arithmetic and copies ran while one was open for 0% of the time, Pallas kernels for 0%

profile of v1, /device:TPU:0, one launch (start us, length us, event | category | flops | bytes accessed | tf_op | source)
XLA Modules:
  0.0 336.4 jit_solution(13763494038128599305)
XLA Ops:
  7.2 0.0 all-gather.4.cloned.1.call-start
  7.2 0.7 all-gather.4.cloned.1.call-update
  7.9 33.2 %all_gather.18 = bf16[1024,256]{1,0:T(8,128)(2,1)S(1)} all-gather(bf16[128,256]{1,0:T(8,128)(2,1)} %param.3), channel_id=1, replica_groups=mesh['batch'=4,'proto'=8] {'proto'}, dimensions={0}, use_global_device_ids=true | all-gather | bytes 589824 | tf_op jit(solution)/shard_map/all_gather | solution.py:28
  41.1 0.2 multiply_reduce_fusion.1
  41.4 5.4 %all-gather.4.cloned.1.call-done = bf16[256,8192]{1,0:T(8,128)(2,1)} async-done(((bf16[64,8192]{1,0:T(8,128)(2,1)}), bf16[256,8192]{1,0:T(8,128)(2,1)}) %all-gather.4.cloned.1.call-update) | async-done | bytes 4194320 | tf_op jit(solution)/shard_map/all_gather | solution.py:31
  46.7 3.1 multiply_reduce_fusion
  49.8 17.7 %fusion.16 = (f32[8192]{0:T(1024)S(1)}, f32[1024,8192]{1,0:T(8,128)}) fusion(f32[8192]{0:T(1024)S(1)} %add_sqrt_fusion, f32[1024]{0:T(1024)S(1)} %add_sqrt_fusion.1, bf16[1024,256]{1,0:T(8,128)(2,1)S(1)} %all_gather.18, bf16[256,8192]{1,0:T(8,128)(2,1)} %all-gather.4.cloned.1.call-done), kind=kOutput, calls=%fused_computation.28 | convolution fusion | flops 4328513536 | bytes 38342656 | tf_op jit(solution)/shard_map/dot_general | solution.py:33
  67.5 10.4 %psum.42 = f32[8192]{0:T(1024)S(1)} all-reduce(f32[8192]{0:T(1024)S(1)} %get-tuple-element.9), channel_id=1, replica_groups=mesh['batch'=4,'proto'=8] {'batch'}, use_global_device_ids=true, to_apply=%region_3.0 | all-reduce | flops 8192 | bytes 65536 | tf_op jit(solution)/shard_map/psum | solution.py:19
  77.9 12.2 %divide_reduce_fusion = f32[1024]{0:T(1024)S(1)} fusion(f32[1024,8192]{1,0:T(8,128)} %get-tuple-element.10, f32[8192]{0:T(1024)S(1)} %psum.42), kind=kLoop, calls=%fused_computation.16 | loop fusion | flops 16776192 | bytes 33591296 | tf_op jit(solution)/shard_map/reduce_sum | solution.py:24
  90.1 30.8 %all-gather = f32[8192]{0:T(1024)S(1)} all-gather(f32[1024]{0:T(1024)S(1)} %divide_reduce_fusion), channel_id=2, replica_groups=mesh['batch'=4,'proto'=8] {'proto'}, dimensions={0}, use_global_device_ids=true | all-gather | bytes 36864 | tf_op jit(solution)/shard_map/all_gather | solution.py:13
  121.0 14.1 %fusion.11 = f32[8192]{0:T(1024)S(1)} fusion(f32[1024,8192]{1,0:T(8,128)} %get-tuple-element.10, f32[1024]{0:T(1024)S(1)} %reduce_sum.112, f32[8192]{0:T(1024)S(1)} %psum.42), kind=kLoop, calls=%fused_computation.17 | loop fusion | flops 25157632 | bytes 33624064 | tf_op jit(solution)/shard_map/reduce_sum | solution.py:19
  135.1 10.3 %psum.43 = f32[8192]{0:T(1024)S(1)} all-reduce(f32[8192]{0:T(1024)S(1)} %fusion.11), channel_id=1, replica_groups=mesh['batch'=4,'proto'=8] {'batch'}, use_global_device_ids=true, to_apply=%region_7.0 | all-reduce | flops 8192 | bytes 65536 | tf_op jit(solution)/shard_map/psum | solution.py:19
  145.3 14.1 %fusion.13 = f32[1024]{0:T(1024)S(1)} fusion(f32[1024,8192]{1,0:T(8,128)} %get-tuple-element.10, f32[8192]{0:T(1024)S(1)} %psum.43, f32[1024]{0:T(1024)S(1)} %reduce_sum.112, f32[8192]{0:T(1024)S(1)} %psum.42), kind=kLoop, calls=%fused_computation.19 | loop fusion | flops 33553408 | bytes 33628160 | tf_op jit(solution)/shard_map/reduce_sum | solution.py:24
  159.5 30.6 %all-gather.1 = f32[8192]{0:T(1024)S(1)} all-gather(f32[1024]{0:T(1024)S(1)} %fusion.13), channel_id=3, replica_groups=mesh['batch'=4,'proto'=8] {'proto'}, dimensions={0}, use_global_device_ids=true | all-gather | bytes 36864 | tf_op jit(solution)/shard_map/all_gather | solution.py:13
  190.1 14.5 %fusion.14 = f32[8192]{0:T(1024)S(1)} fusion(f32[1024,8192]{1,0:T(8,128)} %get-tuple-element.10, f32[1024]{0:T(1024)S(1)} %reduce_sum.115, f32[8192]{0:T(1024)S(1)} %psum.43, f32[1024]{0:T(1024)S(1)} %reduce_sum.112, f32[8192]{0:T(1024)S(1)} %psum.42), kind=kLoop, calls=%fused_computation.20 | loop fusion | flops 41934848 | bytes 33660928 | tf_op jit(solution)/shard_map/reduce_sum | solution.py:19
  204.6 10.4 %psum.44 = f32[8192]{0:T(1024)S(1)} all-reduce(f32[8192]{0:T(1024)S(1)} %fusion.14), channel_id=1, replica_groups=mesh['batch'=4,'proto'=8] {'batch'}, use_global_device_ids=true, to_apply=%region_11.0 | all-reduce | flops 8192 | bytes 65536 | tf_op jit(solution)/shard_map/psum | solution.py:19
  215.1 28.0 %broadcast_multiply_fusion = (f32[1024,8192]{1,0:T(8,128)}, f32[1024]{0:T(1024)S(1)}) fusion(f32[1024,8192]{1,0:T(8,128)} %get-tuple-element.10, f32[8192]{0:T(1024)S(1)} %psum.44, f32[1024]{0:T(1024)S(1)} %reduce_sum.115, f32[8192]{0:T(1024)S(1)} %psum.43, f32[1024]{0:T(1024)S(1)} %reduce_sum.112, f32[8192]{0:T(1024)S(1)} %psum.42), kind=kLoop, calls=%fused_computation.21 | loop fusion | flops 58719232 | bytes 67219456 | tf_op jit(solution)/shard_map/mul | solution.py:43
  243.1 27.8 %fusion.1 = (f32[2,1024]{1,0:T(2,128)S(1)}, f32[2,1024]{1,0:T(2,128)S(1)}) fusion(bf16[2,1024,8192]{2,1,0:T(8,128)(2,1)} %param.5, f32[1024,8192]{1,0:T(8,128)} %get-tuple-element.7), kind=kLoop, calls=%fused_computation.3 | loop fusion | flops 83881984 | bytes 67125248 | tf_op jit(solution)/shard_map/reduce_sum | solution.py:38
  270.9 37.0 %all-reduce = (f32[1024]{0:T(1024)S(1)}, f32[2,1024]{1,0:T(2,128)S(1)}, f32[2,1024]{1,0:T(2,128)S(1)}) all-reduce(f32[1024]{0:T(1024)S(1)} %get-tuple-element.8, f32[2,1024]{1,0:T(2,128)S(1)} %get-tuple-element.3, f32[2,1024]{1,0:T(2,128)S(1)} %get-tuple-element.2), channel_id=1, replica_groups=mesh['batch'=4,'proto'=8] {'proto'}, use_global_device_ids=true, to_apply=%region_13.0 | all-reduce | flops 5120 | bytes 40960 | tf_op jit(solution)/shard_map/psum | solution.py:44
  307.9 21.1 %fusion.12 = bf16[1024,8192]{1,0:T(8,128)(2,1)} fusion(f32[1024,8192]{1,0:T(8,128)} %get-tuple-element.10, f32[1024]{0:T(1024)S(1)} %get-tuple-element.4, f32[8192]{0:T(1024)S(1)} %psum.44, f32[1024]{0:T(1024)S(1)} %reduce_sum.115, f32[8192]{0:T(1024)S(1)} %psum.43, f32[1024]{0:T(1024)S(1)} %reduce_sum.112, f32[8192]{0:T(1024)S(1)} %psum.42), kind=kLoop, calls=%fused_computation.18 | loop fusion | flops 67108864 | bytes 50442240 | tf_op jit(solution)/shard_map/convert_element_type | solution.py:49
  329.0 0.6 divide_subtract_fusion
  (6 shorter events, 0.1 us)
Async XLA Ops:
  7.2 39.6 %all-gather.4.cloned.1.call-start = ((), (), s32[]{:S(2)}) async-start(), calls=%async_computation | async-start | bytes 5242880 | tf_op jit(solution)/shard_map/all_gather | solution.py:31
Sparse Core Ops, SparseCore 0:
  9.5 37.1 all-gather.3
